TPU v7x, 32 devices: a whole 2x2x4 slice. The times are simulated.
32 devices in a mesh: dev: 32 (over z, y, x, core).
Axes of the slice: x: 2, y: 2, z: 4, core: 2. Of those that a mesh axis runs over, the one named last changes fastest.
Arguments:
- inputs: bfloat16 [65536, 227], P('dev'), may hold values from -6 to 6
- targets: float32 [65536, 227], P('dev'), may hold values from -6 to 6
- geometry: bfloat16 [8192, 4], P('dev'), may hold values from -6 to 6
- land_sea: int32 [65536], P('dev'), may hold values 0 or 1
- level_mask: int32 [65536, 227], P('dev'), may hold values from 0 to 1
- edge_owners: int32 [8192, 2], P('dev'), may hold values from 0 to 31, all different within a row; in each aligned block of 256 rows (0 to 255, 256 to 511, ...) at most 20 rows name the same one
- edge_local: int32 [8192, 2], P('dev'), may hold values from 0 to 2047
- step_count: int32 [1], replicated, may hold values from 1 to 20
- master: float32 [6545408], P('dev'), as said below
- first_moment: float32 [6545408], P('dev'), as said below
- second_moment: float32 [6545408], P('dev'), as said below
- ema: float32 [6545408], P('dev'), as said below
Outputs:
- new_master: float32 [6545408], P('dev')
- new_first: float32 [6545408], P('dev')
- new_second: float32 [6545408], P('dev')
- new_ema: float32 [6545408], P('dev')
- loss: float32 [], replicated
- grad_norm: float32 [], replicated
Inputs may be any that keep to these rules, and one draw needn't show every extreme that they name: `edge_owners`: the two columns of a row differ; within the rows of one device no device is named more than 20 times, and some device is named exactly 20 times. `master`: Finite, of the size of fan-in scaled weights, gains near 1. `first_moment`: Finite, both signs. `second_moment`: Positive. `ema`: Finite, of the size of fan-in scaled weights, gains near 1.
All inputs are finite; a program needn't handle non-finite values. No bound on the sum of `land_sea` on one device may be relied on, other than what follows from the above.
Results may differ from a plain program's by a relative error of at most 0.00045.
The roundings to bfloat16 on the way count: a program that leaves them out, or rounds other values in their place, can miss the bound.
Values may be sent and summed in bfloat16 or wider, within the bound.
A program may use at most 192 MiB of HBM per device.

v0:
```python
import jax
import jax.numpy as jnp
import numpy as np
from jax import lax
from jax.sharding import PartitionSpec as P

LATENT = 512
VARS = 227
GEO = 4
SEA_VARS = 4
LAYERS = 3
PARAMS = 6545408
norm_eps = 1e-05
clip_limit = 0.01
beta_one = 0.9
beta_two = 0.999
adam_eps = 1e-08
learn_rate = 0.03
decay_rate = 0.1
ema_keep = 0.9


def layout(width, variables, geometry, layers):
    shapes = [(variables, width, True), (geometry, width, True)]
    for k in range(layers):
        shapes.append((3 * width, width, True))
        shapes.append((2 * width, width, True))
    shapes.append((width, variables, False))
    segments = []
    offset = 0
    for block_id, (fan_in, fan_out, normed) in enumerate(shapes):
        members = [
            ("w_in", (fan_in, width)),
            ("b_in", (width,)),
            ("w_out", (width, fan_out)),
            ("b_out", (fan_out,)),
        ]
        if normed:
            members = members + [("gain", (fan_out,)), ("shift", (fan_out,))]
        for part_name, part_shape in members:
            entries = int(np.prod(part_shape))
            segments.append((block_id, part_name, part_shape, offset, entries))
            offset += entries
    return (segments, offset)


def unpack(flat, segments):
    blocks = [dict() for k in range(segments[-1][0] + 1)]
    for block_id, part_name, part_shape, offset, entries in segments:
        blocks[block_id][part_name] = flat[offset : offset + entries].reshape(part_shape)
    return blocks


def mlp_forward(params, source):
    pre = jnp.dot(source, params["w_in"], preferred_element_type=jnp.float32) + params[
        "b_in"
    ].astype(jnp.float32)
    act = jax.nn.silu(pre).astype(jnp.bfloat16)
    post = jnp.dot(act, params["w_out"], preferred_element_type=jnp.float32) + params[
        "b_out"
    ].astype(jnp.float32)
    if "gain" in params:
        centred = post - jnp.mean(post, axis=-1, keepdims=True)
        inv_std = lax.rsqrt(jnp.mean(centred * centred, axis=-1, keepdims=True) + norm_eps)
        scaled = centred * inv_std
        result = scaled * params["gain"].astype(jnp.float32) + params["shift"].astype(jnp.float32)
        return (result, (source, pre, act, scaled, inv_std))
    return (post, (source, pre, act, None, None))


def mlp_backward(params, kept, grad_out, need_input):
    source, pre, act, scaled, inv_std = kept
    grads = {}
    if scaled is not None:
        grads["gain"] = jnp.sum(grad_out * scaled, axis=0)
        grads["shift"] = jnp.sum(grad_out, axis=0)
        grad_scaled = grad_out * params["gain"].astype(jnp.float32)
        grad_post = inv_std * (
            grad_scaled
            - jnp.mean(grad_scaled, axis=-1, keepdims=True)
            - scaled * jnp.mean(grad_scaled * scaled, axis=-1, keepdims=True)
        )
    else:
        grad_post = grad_out
    post_low = grad_post.astype(jnp.bfloat16)
    grads["w_out"] = jnp.einsum("ni,nj->ij", act, post_low, preferred_element_type=jnp.float32)
    grads["b_out"] = jnp.sum(post_low.astype(jnp.float32), axis=0)
    grad_act = jnp.einsum(
        "nj,ij->ni", post_low, params["w_out"], preferred_element_type=jnp.float32
    )
    sigma = jax.nn.sigmoid(pre)
    pre_low = (grad_act * sigma * (1.0 + pre * (1.0 - sigma))).astype(jnp.bfloat16)
    grads["w_in"] = jnp.einsum("ni,nj->ij", source, pre_low, preferred_element_type=jnp.float32)
    grads["b_in"] = jnp.sum(pre_low.astype(jnp.float32), axis=0)
    grad_source = None
    if need_input:
        grad_source = jnp.einsum(
            "nj,ij->ni", pre_low, params["w_in"], preferred_element_type=jnp.float32
        )
    return (grad_source, grads)


def make_routes(edge_owners, edge_local):
    devices = lax.axis_size("dev")
    edges_here = edge_owners.shape[0]
    capacity = 5 * edges_here // (2 * devices)
    wanted_owner = edge_owners.reshape(-1)
    wanted_local = edge_local.reshape(-1)
    one_hot = (wanted_owner[:, None] == jnp.arange(devices, dtype=jnp.int32)[None, :]).astype(
        jnp.int32
    )
    ranking = jnp.sum((jnp.cumsum(one_hot, axis=0) - 1) * one_hot, axis=1)
    position = wanted_owner * capacity + ranking
    asking = jnp.zeros((devices * capacity,), jnp.int32).at[position].set(wanted_local + 1)
    served = lax.all_to_all(
        asking.reshape(devices, capacity), "dev", split_axis=0, concat_axis=0, tiled=True
    ).reshape(-1)
    valid = served > 0
    served_rows = jnp.maximum(served - 1, 0)
    return (served_rows, valid, position, position[1::2], devices, capacity)


def layer_forward(edge_params, node_params, node, edge, routes):
    served_rows, valid, position, recv_pos, devices, capacity = routes
    node_low = node.astype(jnp.bfloat16)
    outgoing = jnp.where(valid[:, None], node_low[served_rows], jnp.zeros((), jnp.bfloat16))
    arrived = lax.all_to_all(
        outgoing.reshape(devices, capacity, LATENT), "dev", split_axis=0, concat_axis=0, tiled=True
    ).reshape(-1, LATENT)
    gathered = arrived[position].reshape(edge.shape[0], 2 * LATENT)
    edge_in = jnp.concatenate([edge.astype(jnp.bfloat16), gathered], axis=1)
    edge_out, edge_kept = mlp_forward(edge_params, edge_in)
    edge_new = edge + edge_out
    buffer = (
        jnp.zeros((devices * capacity, LATENT), jnp.bfloat16)
        .at[recv_pos]
        .set(edge_new.astype(jnp.bfloat16))
    )
    landed = lax.all_to_all(
        buffer.reshape(devices, capacity, LATENT), "dev", split_axis=0, concat_axis=0, tiled=True
    ).reshape(-1, LATENT)
    landed = jnp.where(valid[:, None], landed.astype(jnp.float32), 0.0)
    summed = jnp.zeros(node.shape, jnp.float32).at[served_rows].add(landed)
    node_in = jnp.concatenate([node_low, summed.astype(jnp.bfloat16)], axis=1)
    node_out, node_kept = mlp_forward(node_params, node_in)
    return (node + node_out, edge_new, (edge_kept, node_kept))


def layer_backward(edge_params, node_params, kept, grad_node, grad_edge, routes):
    served_rows, valid, position, recv_pos, devices, capacity = routes
    edge_kept, node_kept = kept
    node_source, node_grads = mlp_backward(node_params, node_kept, grad_node, True)
    grad_total = grad_node + node_source[:, :LATENT]
    summed_low = node_source[:, LATENT:].astype(jnp.bfloat16)
    outgoing = jnp.where(valid[:, None], summed_low[served_rows], jnp.zeros((), jnp.bfloat16))
    returned = lax.all_to_all(
        outgoing.reshape(devices, capacity, LATENT), "dev", split_axis=0, concat_axis=0, tiled=True
    ).reshape(-1, LATENT)
    edge_total = grad_edge + returned[recv_pos].astype(jnp.float32)
    edge_source, edge_grads = mlp_backward(edge_params, edge_kept, edge_total, True)
    edge_prev = edge_total + edge_source[:, :LATENT]
    gathered_low = edge_source[:, LATENT:].reshape(-1, LATENT).astype(jnp.bfloat16)
    buffer = jnp.zeros((devices * capacity, LATENT), jnp.bfloat16).at[position].set(gathered_low)
    landed = lax.all_to_all(
        buffer.reshape(devices, capacity, LATENT), "dev", split_axis=0, concat_axis=0, tiled=True
    ).reshape(-1, LATENT)
    landed = jnp.where(valid[:, None], landed.astype(jnp.float32), 0.0)
    grad_total = grad_total.at[served_rows].add(landed)
    return (grad_total, edge_prev, edge_grads, node_grads)


def local(
    inputs,
    targets,
    geometry,
    land_sea,
    level_mask,
    edge_owners,
    edge_local,
    step_count,
    master,
    first_moment,
    second_moment,
    ema,
):
    segments, total = layout(LATENT, VARS, GEO, LAYERS)
    full_weights = lax.all_gather(master.astype(jnp.bfloat16), "dev", axis=0, tiled=True)
    blocks = unpack(full_weights, segments)
    routes = make_routes(edge_owners, edge_local)
    node, enc_kept = mlp_forward(blocks[0], inputs)
    edge, geo_kept = mlp_forward(blocks[1], geometry)
    layer_kept = []
    for k in range(LAYERS):
        node, edge, kept = layer_forward(blocks[2 + 2 * k], blocks[3 + 2 * k], node, edge, routes)
        layer_kept.append(kept)
    decoded, dec_kept = mlp_forward(blocks[2 + 2 * LAYERS], node.astype(jnp.bfloat16))
    pred = inputs.astype(jnp.float32) + decoded
    ocean = (jnp.arange(VARS) < SEA_VARS).astype(jnp.float32)
    mask = level_mask.astype(jnp.float32) * (
        1.0 - land_sea.astype(jnp.float32)[:, None] * ocean[None, :]
    )
    residual = pred - targets
    error_sum, count = lax.psum((jnp.sum(mask * residual * residual), jnp.sum(mask)), "dev")
    divisor = jnp.maximum(count, 1.0)
    loss = error_sum / divisor
    grad_pred = 2.0 * mask * residual / divisor
    grads = [None] * (3 + 2 * LAYERS)
    dec_source, grads[2 + 2 * LAYERS] = mlp_backward(
        blocks[2 + 2 * LAYERS], dec_kept, grad_pred, True
    )
    grad_node = dec_source
    grad_edge = jnp.zeros(edge.shape, jnp.float32)
    for k in reversed(range(LAYERS)):
        grad_node, grad_edge, grads[2 + 2 * k], grads[3 + 2 * k] = layer_backward(
            blocks[2 + 2 * k], blocks[3 + 2 * k], layer_kept[k], grad_node, grad_edge, routes
        )
    unused, grads[1] = mlp_backward(blocks[1], geo_kept, grad_edge, False)
    unused, grads[0] = mlp_backward(blocks[0], enc_kept, grad_node, False)
    pieces = [
        grads[block_id][part_name].reshape(-1)
        for block_id, part_name, part_shape, offset, entries in segments
    ]
    pieces.append(jnp.zeros((PARAMS - total,), jnp.float32))
    flat_grad = jnp.concatenate(pieces)
    summed_grad = lax.psum(flat_grad, "dev")
    share = master.shape[0]
    own_grad = lax.dynamic_slice_in_dim(summed_grad, lax.axis_index("dev") * share, share)
    squares = jnp.sum(summed_grad * summed_grad)
    grad_norm = jnp.sqrt(squares)
    clipped = own_grad * jnp.minimum(1.0, clip_limit / grad_norm)
    step = step_count[0].astype(jnp.float32)
    new_first = beta_one * first_moment + (1.0 - beta_one) * clipped
    new_second = beta_two * second_moment + (1.0 - beta_two) * clipped * clipped
    first_hat = new_first / (1.0 - beta_one**step)
    second_hat = new_second / (1.0 - beta_two**step)
    new_master = master - learn_rate * (
        first_hat / (jnp.sqrt(second_hat) + adam_eps) + decay_rate * master
    )
    new_ema = ema_keep * ema + (1.0 - ema_keep) * new_master
    return (new_master, new_first, new_second, new_ema, loss, grad_norm)


def solution(mesh):
    in_specs = (
        P("dev", None),
        P("dev", None),
        P("dev", None),
        P("dev"),
        P("dev", None),
        P("dev", None),
        P("dev", None),
        P(),
        P("dev"),
        P("dev"),
        P("dev"),
        P("dev"),
    )
    out_specs = (P("dev"), P("dev"), P("dev"), P("dev"), P(), P())
    return jax.shard_map(local, mesh=mesh, in_specs=in_specs, out_specs=out_specs, check_vma=False)
```

profile of v0, /device:TPU:0, one launch (start us, length us, event | category | flops | bytes accessed | tf_op | source)
XLA Modules:
  0.0 1851.5 jit_solution(10392052022695157452)
XLA Ops:
  21.7 7.6 all-to-all-start
  37.6 138.8 %all-gather.3.cloned.1.call-done = bf16[32,1,204544]{2,1,0:T(2,128)(2,1)} async-done(((bf16[1,1,204544]{2,1,0:T(2,128)(2,1)}), bf16[32,1,204544]{2,1,0:T(2,128)(2,1)}) %all-gather.3.cloned.1.call-update) | async-done | bytes 13090832 | tf_op jit(solution)/shard_map/all_gather | solution.py:187
  176.4 277.2 %reduce = bf16[32,204544]{1,0:T(8,128)(2,1)} reduce(bf16[32,1,204544]{2,1,0:T(2,128)(2,1)} %all-gather.3.cloned.1.call-done, bf16[]{:T(256)} %constant.119), dimensions={1}, to_apply=%all-gather.reduce_sub_computation | reduce | bytes 26181634 | tf_op jit(solution)/shard_map/all_gather | solution.py:187
  453.6 23.7 %reshape.887 = bf16[6545408]{0:T(1024)(128)(2,1)} reshape(bf16[32,204544]{1,0:T(8,128)(2,1)} %reduce) | data formatting | bytes 26181632
  520.1 16.8 all-to-all-done.1
  558.8 12.6 all-to-all-done.2
  571.6 10.2 scatter_custom_fusion.2
  618.2 17.0 all-to-all-done.3
  653.0 18.0 all-to-all-done.4
  671.2 10.1 scatter_custom_fusion.4
  686.1 6.8 multiply_convert_fusion.11
  716.1 17.3 all-to-all-done.5
  754.6 14.6 all-to-all-done.6
  770.5 10.5 scatter_custom_fusion.6
  785.8 6.9 multiply_convert_fusion.10
  808.9 39.5 %all-reduce = (f32[]{:T(128)}, f32[]{:T(128)}) all-reduce(f32[]{:T(128)} %get-tuple-element.19, f32[]{:T(128)} %get-tuple-element.18), channel_id=1, replica_groups=mesh['dev'=32] {'dev'}, use_global_device_ids=true, to_apply=%region_27.28 | all-reduce | flops 2 | bytes 16 | tf_op jit(solution)/shard_map/psum | solution.py:203
  898.8 16.7 all-to-all-done.7
  951.1 12.4 scatter_custom_fusion.8
  1051.0 12.3 scatter_custom_fusion.10
  1141.4 12.1 all-to-all-done.12
  1153.6 12.2 scatter_custom_fusion.12
  1191.5 231.7 %concatenate.27 = f32[6545408]{0:T(1024)} concatenate(f32[116224]{0:T(1024)} %reshape.644, f32[512]{0:T(512)S(1)} %get-tuple-element.150, f32[262144]{0:T(1024)} %bitcast.184, f32[512]{0:T(512)S(1)} %get-tuple-element.59, f32[512]{0:T(512)S(1)} %get-tuple-element.12, f32[512]{0:T(512)S(1)} %reduce_sum.668, f32[2048]{0:T(1024)S(1)} %bitcast.185, f32[512]{0:T(512)S(1)} %get-tuple-element.152, ...), dimensions={0} | concatenate | bytes 52363264 | tf_op jit(solution)/shard_map/concatenate | solution.py:224
  1424.7 402.6 %all-reduce.3.cloned.1.call-done = f32[6545408]{0:T(1024)} async-done(((f32[6545408]{0:T(1024)}), f32[6545408]{0:T(1024)}) %all-reduce.3.cloned.1.call-update) | async-done | bytes 26181648 | tf_op jit(solution)/shard_map/psum | solution.py:225
  1827.3 10.4 multiply_reduce_fusion
  (724 shorter events, 490.9 us)
Async XLA Ops:
  7.2 509.1 %copy-start = (bf16[256,4]{0,1:T(4,128)(2,1)S(1)}, bf16[256,4]{0,1:T(4,128)(2,1)}, u32[]{:S(2)}) copy-start(bf16[256,4]{0,1:T(4,128)(2,1)} %param.14) | copy-start | bytes 6148
  7.2 169.3 %all-gather.3.cloned.1.call-start = ((), (), s32[]{:S(2)}) async-start(), calls=%async_computation.14 | async-start | bytes 26999808 | tf_op jit(solution)/shard_map/all_gather | solution.py:187
  21.7 14.7 all-to-all-start
  37.6 416.1 %copy-start.169 = (s32[640]{0:T(1024)}, s32[640]{0:T(1024)S(1)}, u32[]{:S(2)}) copy-start(s32[640]{0:T(1024)S(1)} %reshape.782) | copy-start | bytes 7684
  37.6 471.9 %copy-start.118 = (s32[1024]{0:T(1024)}, s32[1024]{0:T(1024)S(1)}, u32[]{:S(2)}) copy-start(s32[1024]{0:T(1024)S(1)} %pad_clamp_fusion.2) | copy-start | bytes 12292
  502.4 94.3 %copy-start.106 = (f32[2048]{0:T(1024)}, f32[2048]{0:T(1024)S(1)}, u32[]{:S(2)}) copy-start(f32[2048]{0:T(1024)S(1)} %broadcast_multiply_fusion.11) | copy-start | bytes 24580
  513.5 23.4 %all-to-all-start.1 = ((bf16[32,20,512]{2,1,0:T(8,128)(2,1)}), bf16[32,20,512]{2,1,0:T(8,128)(2,1)S(1)}, u32[]{:S(2)}, u32[]{:S(2)}) async-start(bf16[32,20,512]{2,1,0:T(8,128)(2,1)} %broadcast_select_fusion.5), calls=%async_computation.1 | async-start | bytes 1572864 | tf_op jit(solution)/shard_map/all_to_all | solution.py:127
  543.9 95.5 %copy-start.73 = (bf16[256,512]{1,0:T(8,128)(2,1)}, bf16[256,512]{1,0:T(8,128)(2,1)S(1)}, u32[]{:S(2)}) copy-start(bf16[256,512]{1,0:T(8,128)(2,1)S(1)} %get-tuple-element.65) | copy-start | bytes 786436
  546.8 24.6 %all-to-all-start.2 = ((bf16[32,20,512]{2,1,0:T(8,128)(2,1)}), bf16[32,20,512]{2,1,0:T(8,128)(2,1)S(1)}, u32[]{:S(2)}, u32[]{:S(2)}) async-start(bf16[32,20,512]{2,1,0:T(8,128)(2,1)} %reshape.630), calls=%async_computation.2 | async-start | bytes 1572864 | tf_op jit(solution)/shard_map/all_to_all | solution.py:139
  610.9 24.4 %all-to-all-start.3 = ((bf16[32,20,512]{2,1,0:T(8,128)(2,1)}), bf16[32,20,512]{2,1,0:T(8,128)(2,1)}, u32[]{:S(2)}, u32[]{:S(2)}) async-start(bf16[32,20,512]{2,1,0:T(8,128)(2,1)} %broadcast_select_fusion.4), calls=%async_computation.3 | async-start | bytes 1572864 | tf_op jit(solution)/shard_map/all_to_all | solution.py:127
  646.8 24.2 %all-to-all-start.4 = ((bf16[32,20,512]{2,1,0:T(8,128)(2,1)}), bf16[32,20,512]{2,1,0:T(8,128)(2,1)S(1)}, u32[]{:S(2)}, u32[]{:S(2)}) async-start(bf16[32,20,512]{2,1,0:T(8,128)(2,1)} %reshape.633), calls=%async_computation.4 | async-start | bytes 1572864 | tf_op jit(solution)/shard_map/all_to_all | solution.py:139
  709.1 24.2 %all-to-all-start.5 = ((bf16[32,20,512]{2,1,0:T(8,128)(2,1)}), bf16[32,20,512]{2,1,0:T(8,128)(2,1)S(1)}, u32[]{:S(2)}, u32[]{:S(2)}) async-start(bf16[32,20,512]{2,1,0:T(8,128)(2,1)} %broadcast_select_fusion.3), calls=%async_computation.5 | async-start | bytes 1572864 | tf_op jit(solution)/shard_map/all_to_all | solution.py:127
  744.9 24.4 %all-to-all-start.6 = ((bf16[32,20,512]{2,1,0:T(8,128)(2,1)}), bf16[32,20,512]{2,1,0:T(8,128)(2,1)}, u32[]{:S(2)}, u32[]{:S(2)}) async-start(bf16[32,20,512]{2,1,0:T(8,128)(2,1)} %reshape.636), calls=%async_computation.6 | async-start | bytes 1572864 | tf_op jit(solution)/shard_map/all_to_all | solution.py:139
  890.4 25.2 %all-to-all-start.7 = ((bf16[32,20,512]{2,1,0:T(8,128)(2,1)}), bf16[32,20,512]{2,1,0:T(8,128)(2,1)}, u32[]{:S(2)}, u32[]{:S(2)}) async-start(bf16[32,20,512]{2,1,0:T(8,128)(2,1)} %broadcast_select_fusion.2), calls=%async_computation.7 | async-start | bytes 1572864 | tf_op jit(solution)/shard_map/all_to_all | solution.py:156
  925.5 24.4 %all-to-all-start.8 = ((bf16[32,20,512]{2,1,0:T(8,128)(2,1)}), bf16[32,20,512]{2,1,0:T(8,128)(2,1)}, u32[]{:S(2)}, u32[]{:S(2)}) async-start(bf16[32,20,512]{2,1,0:T(8,128)(2,1)} %reshape.639), calls=%async_computation.8 | async-start | bytes 1572864 | tf_op jit(solution)/shard_map/all_to_all | solution.py:164
  991.7 24.4 %all-to-all-start.9 = ((bf16[32,20,512]{2,1,0:T(8,128)(2,1)}), bf16[32,20,512]{2,1,0:T(8,128)(2,1)S(1)}, u32[]{:S(2)}, u32[]{:S(2)}) async-start(bf16[32,20,512]{2,1,0:T(8,128)(2,1)} %broadcast_select_fusion.1), calls=%async_computation.9 | async-start | bytes 1572864 | tf_op jit(solution)/shard_map/all_to_all | solution.py:156
  1026.4 24.4 %all-to-all-start.10 = ((bf16[32,20,512]{2,1,0:T(8,128)(2,1)}), bf16[32,20,512]{2,1,0:T(8,128)(2,1)S(1)}, u32[]{:S(2)}, u32[]{:S(2)}) async-start(bf16[32,20,512]{2,1,0:T(8,128)(2,1)} %reshape.641), calls=%async_computation.10 | async-start | bytes 1572864 | tf_op jit(solution)/shard_map/all_to_all | solution.py:164
  1093.5 24.8 %all-to-all-start.11 = ((bf16[32,20,512]{2,1,0:T(8,128)(2,1)}), bf16[32,20,512]{2,1,0:T(8,128)(2,1)}, u32[]{:S(2)}, u32[]{:S(2)}) async-start(bf16[32,20,512]{2,1,0:T(8,128)(2,1)} %broadcast_select_fusion), calls=%async_computation.11 | async-start | bytes 1572864 | tf_op jit(solution)/shard_map/all_to_all | solution.py:156
  1129.2 24.3 %all-to-all-start.12 = ((bf16[32,20,512]{2,1,0:T(8,128)(2,1)}), bf16[32,20,512]{2,1,0:T(8,128)(2,1)S(1)}, u32[]{:S(2)}, u32[]{:S(2)}) async-start(bf16[32,20,512]{2,1,0:T(8,128)(2,1)} %reshape.643), calls=%async_computation.12 | async-start | bytes 1572864 | tf_op jit(solution)/shard_map/all_to_all | solution.py:164
  1132.8 694.5 %all-reduce.3.cloned.1.call-start = ((), (), s32[]{:S(2)}) async-start(), calls=%async_computation.13 | async-start | bytes 52363264 | tf_op jit(solution)/shard_map/psum | solution.py:225
  1424.6 413.8 %copy-start.50 = (f32[204544]{0:T(1024)S(1)}, f32[204544]{0:T(1024)}, u32[]{:S(2)}) copy-start(f32[204544]{0:T(1024)} %param.20) | copy-start | bytes 2454532
  1424.6 413.8 %copy-start.88 = (f32[204544]{0:T(1024)S(1)}, f32[204544]{0:T(1024)}, u32[]{:S(2)}) copy-start(f32[204544]{0:T(1024)} %param.23) | copy-start | bytes 2454532
  1424.7 413.8 %copy-start.89 = (f32[204544]{0:T(1024)S(1)}, f32[204544]{0:T(1024)}, u32[]{:S(2)}) copy-start(f32[204544]{0:T(1024)} %param.22) | copy-start | bytes 2454532
  1424.7 413.8 %copy-start.90 = (f32[204544]{0:T(1024)S(1)}, f32[204544]{0:T(1024)}, u32[]{:S(2)}) copy-start(f32[204544]{0:T(1024)} %param.21) | copy-start | bytes 2454532
  (207 other events, 1224.7 us)
Sparse Core Ops, SparseCore 0:
  14.0 162.4 all-gather.2
  1423.4 403.9 all-reduce.2
where the time goes:
time: 1870 us; the launch traced here: 1850 us
  waiting for transfers between devices  693 us (37%)
  local copies, waits for them, and re-layouts  482 us (26%)
  other arithmetic  449 us (24%)
  matrix products  112 us (6%)
  starting transfers between devices  53.1 us (3%)
  blocking collectives  39.5 us (2%)
  between operations  22.6 us (1%)
    psum x1, waiting for transfers between devices, local(): summed_grad = lax.psum(flat_grad, 'dev')  403 us
    all_gather x1, other arithmetic, local(): lax.all_gather(master.astype(jnp.bfloat16), 'dev', axis=0, tiled=True)  277 us
    concatenate x1, local copies, waits for them, and re-layouts, local(): flat_grad = jnp.concatenate(pieces)  232 us
    all_gather x1, waiting for transfers between devices, local(): lax.all_gather(master.astype(jnp.bfloat16), 'dev', axis=0, tiled=True)  139 us
    unnamed x451, local copies, waits for them, and re-layouts  92.5 us
    all_to_all x3, waiting for transfers between devices, layer_forward(): lax.all_to_all(outgoing.reshape(devices, capacity, LATENT), 'dev', split_...  51.1 us
    all_to_all x3, waiting for transfers between devices, layer_forward(): lax.all_to_all(buffer.reshape(devices, capacity, LATENT), 'dev', split_ax...  45.3 us
    psum x1, blocking collectives, local(): lax.psum((jnp.sum(mask * residual * residual), jnp.sum(mask)), 'dev')  39.5 us
  transfers between devices with their start and end apart: 15, of which 15 were waited for; matrix products, arithmetic and copies ran while one was open for 6% of the time, Pallas kernels for 0%

commit v1 on v0

--- a/solution.py
+++ b/solution.py
@@ -222,7 +222,11 @@
     ]
     pieces.append(jnp.zeros((PARAMS - total,), jnp.float32))
     flat_grad = jnp.concatenate(pieces)
-    summed_grad = lax.psum(flat_grad, "dev")
+    summed_grad = flat_grad
+    for hop in (1, 2, 4, 8, 16):
+        summed_grad = summed_grad + lax.ppermute(
+            summed_grad, "dev", [(dev, dev ^ hop) for dev in range(32)]
+        )
     share = master.shape[0]
     own_grad = lax.dynamic_slice_in_dim(summed_grad, lax.axis_index("dev") * share, share)
     squares = jnp.sum(summed_grad * summed_grad)

time: 1870 us -> 4440 us (2.37)
  waiting for transfers between devices: 693 us -> 3130 us
  other arithmetic: 449 us -> 572 us
    ppermute x0 -> x5, waiting for transfers between devices: none -> 2840 us  [local(): lax.ppermute(summed_grad, 'dev', [(dev, dev ^ hop) for dev in range(32)])]
    psum x1 -> x0, waiting for transfers between devices: 403 us -> none  [local(): summed_grad = lax.psum(flat_grad, 'dev')]
    add x0 -> x4, other arithmetic: none -> 106 us  [local(): summed_grad + lax.ppermute(summed_grad, 'dev', [(dev, dev ^ hop) for dev...]
  transfers between devices with their start and end apart: 15 -> 19, of which waited for: 15 -> 19; matrix products, arithmetic and copies ran while one was open for 6% -> 2% of each run, Pallas kernels for 0% -> 0%
where the time goes in v1:
time: 4440 us; the launch traced here: 4420 us
  waiting for transfers between devices  3130 us (70%)
  other arithmetic  572 us (13%)
  local copies, waits for them, and re-layouts  481 us (11%)
  matrix products  112 us (3%)
  starting transfers between devices  59.6 us (1%)
    ppermute x5, waiting for transfers between devices, local(): lax.ppermute(summed_grad, 'dev', [(dev, dev ^ hop) for dev in range(32)])  2840 us
    all_gather x1, other arithmetic, local(): lax.all_gather(master.astype(jnp.bfloat16), 'dev', axis=0, tiled=True)  277 us
    concatenate x1, local copies, waits for them, and re-layouts, local(): flat_grad = jnp.concatenate(pieces)  232 us
    all_gather x1, waiting for transfers between devices, local(): lax.all_gather(master.astype(jnp.bfloat16), 'dev', axis=0, tiled=True)  139 us
    add x4, other arithmetic, local(): summed_grad + lax.ppermute(summed_grad, 'dev', [(dev, dev ^ hop) for dev...  106 us
    unnamed x451, local copies, waits for them, and re-layouts  91.3 us
  transfers between devices with their start and end apart: 19, of which 19 were waited for; matrix products, arithmetic and copies ran while one was open for 2% of the time, Pallas kernels for 0%

profile of v1, /device:TPU:0, one launch (start us, length us, event | category | flops | bytes accessed | tf_op | source)
XLA Modules:
  0.0 4422.0 jit_solution(17384175065957021259)
XLA Ops:
  37.6 138.8 %all-gather.3.cloned.1.call-done = bf16[32,1,204544]{2,1,0:T(2,128)(2,1)} async-done(((bf16[1,1,204544]{2,1,0:T(2,128)(2,1)}), bf16[32,1,204544]{2,1,0:T(2,128)(2,1)}) %all-gather.3.cloned.1.call-update) | async-done | bytes 13090832 | tf_op jit(solution)/shard_map/all_gather | solution.py:187
  176.4 277.2 %reduce = bf16[32,204544]{1,0:T(8,128)(2,1)} reduce(bf16[32,1,204544]{2,1,0:T(2,128)(2,1)} %all-gather.3.cloned.1.call-done, bf16[]{:T(256)} %constant.119), dimensions={1}, to_apply=%all-gather.reduce_sub_computation | reduce | bytes 26181634 | tf_op jit(solution)/shard_map/all_gather | solution.py:187
  453.7 23.7 reshape.887
  520.1 16.8 all-to-all-done.1
  558.9 12.6 all-to-all-done.2
  616.9 17.0 all-to-all-done.3
  651.7 18.0 all-to-all-done.4
  714.8 17.3 all-to-all-done.5
  753.3 14.6 all-to-all-done.6
  807.6 39.5 all-reduce
  897.6 16.7 all-to-all-done.7
  949.9 12.5 scatter_custom_fusion.8
  1049.8 12.3 scatter_custom_fusion.10
  1190.6 231.6 %concatenate.27 = f32[6545408]{0:T(1024)} concatenate(f32[116224]{0:T(1024)} %reshape.644, f32[512]{0:T(512)S(1)} %get-tuple-element.152, f32[262144]{0:T(1024)} %bitcast.184, f32[512]{0:T(512)S(1)} %get-tuple-element.61, f32[512]{0:T(512)S(1)} %get-tuple-element.12, f32[512]{0:T(512)S(1)} %reduce_sum.668, f32[2048]{0:T(1024)S(1)} %bitcast.185, f32[512]{0:T(512)S(1)} %get-tuple-element.154, ...), dimensions={0} | concatenate | bytes 52363264 | tf_op jit(solution)/shard_map/concatenate | solution.py:224
  1422.3 38.9 collective-permute-done
  1461.2 26.5 add.603
  1489.2 562.6 %collective-permute-done.1 = f32[6545408]{0:T(1024)} collective-permute-done((f32[6545408]{0:T(1024)}, f32[6545408]{0:T(1024)}, u32[]{:S(2)}, u32[]{:S(2)}) %collective-permute-start.1) | collective-permute-done | bytes 26181664 | tf_op jit(solution)/shard_map/ppermute | solution.py:227
  2051.8 26.5 add.604
  2079.8 561.8 %collective-permute-done.2 = f32[6545408]{0:T(1024)} collective-permute-done((f32[6545408]{0:T(1024)}, f32[6545408]{0:T(1024)}, u32[]{:S(2)}, u32[]{:S(2)}) %collective-permute-start.2) | collective-permute-done | bytes 26181664 | tf_op jit(solution)/shard_map/ppermute | solution.py:227
  2641.6 26.5 add.605
  2669.5 561.0 %collective-permute-done.3 = f32[6545408]{0:T(1024)} collective-permute-done((f32[6545408]{0:T(1024)}, f32[6545408]{0:T(1024)}, u32[]{:S(2)}, u32[]{:S(2)}) %collective-permute-start.3) | collective-permute-done | bytes 26181664 | tf_op jit(solution)/shard_map/ppermute | solution.py:227
  3230.4 26.5 add.606
  3260.4 1119.9 %collective-permute-done.4 = f32[6545408]{0:T(1024)} collective-permute-done((f32[6545408]{0:T(1024)}, f32[6545408]{0:T(1024)}, u32[]{:S(2)}, u32[]{:S(2)}) %collective-permute-start.4) | collective-permute-done | bytes 26181664 | tf_op jit(solution)/shard_map/ppermute | solution.py:227
  4380.3 27.8 multiply_reduce_fusion
  (735 shorter events, 572.7 us)
Async XLA Ops:
  7.2 509.1 %copy-start = (bf16[256,4]{0,1:T(4,128)(2,1)S(1)}, bf16[256,4]{0,1:T(4,128)(2,1)}, u32[]{:S(2)}) copy-start(bf16[256,4]{0,1:T(4,128)(2,1)} %param.14) | copy-start | bytes 6148
  7.2 169.3 %all-gather.3.cloned.1.call-start = ((), (), s32[]{:S(2)}) async-start(), calls=%async_computation.13 | async-start | bytes 26999808 | tf_op jit(solution)/shard_map/all_gather | solution.py:187
  21.7 14.7 all-to-all-start
  513.5 23.4 all-to-all-start.1
  546.8 24.6 all-to-all-start.2
  609.6 24.4 all-to-all-start.3
  645.5 24.2 all-to-all-start.4
  707.8 24.2 all-to-all-start.5
  743.6 24.4 all-to-all-start.6
  889.2 25.2 all-to-all-start.7
  924.3 24.4 all-to-all-start.8
  990.5 24.4 all-to-all-start.9
  1025.2 24.5 all-to-all-start.10
  1092.4 24.8 all-to-all-start.11
  1128.1 24.4 all-to-all-start.12
  1422.3 38.9 collective-permute-start
  1487.7 564.1 %collective-permute-start.1 = (f32[6545408]{0:T(1024)}, f32[6545408]{0:T(1024)}, u32[]{:S(2)}, u32[]{:S(2)}) collective-permute-start(f32[6545408]{0:T(1024)} %add.603), channel_id=1, source_target_pairs={{0,2},{1,3},{2,0},{3,1},{4,6},{5,7},{6,4},{7,5},{8,10},{9,11},{10,... | collective-permute-start | bytes 78544904 | tf_op jit(solution)/shard_map/ppermute | solution.py:227
  2078.3 563.3 %collective-permute-start.2 = (f32[6545408]{0:T(1024)}, f32[6545408]{0:T(1024)}, u32[]{:S(2)}, u32[]{:S(2)}) collective-permute-start(f32[6545408]{0:T(1024)} %add.604), channel_id=1, source_target_pairs={{0,4},{1,5},{2,6},{3,7},{4,0},{5,1},{6,2},{7,3},{8,12},{9,13},{10,... | collective-permute-start | bytes 78544904 | tf_op jit(solution)/shard_map/ppermute | solution.py:227
  2668.1 562.4 %collective-permute-start.3 = (f32[6545408]{0:T(1024)}, f32[6545408]{0:T(1024)}, u32[]{:S(2)}, u32[]{:S(2)}) collective-permute-start(f32[6545408]{0:T(1024)} %add.605), channel_id=1, source_target_pairs={{0,8},{1,9},{2,10},{3,11},{4,12},{5,13},{6,14},{7,15},{8,0},{9,1},... | collective-permute-start | bytes 78544904 | tf_op jit(solution)/shard_map/ppermute | solution.py:227
  3256.9 1123.4 %collective-permute-start.4 = (f32[6545408]{0:T(1024)}, f32[6545408]{0:T(1024)}, u32[]{:S(2)}, u32[]{:S(2)}) collective-permute-start(f32[6545408]{0:T(1024)} %add.606), channel_id=1, source_target_pairs={{0,16},{1,17},{2,18},{3,19},{4,20},{5,21},{6,22},{7,23},{8,24},{9,... | collective-permute-start | bytes 78544904 | tf_op jit(solution)/shard_map/ppermute | solution.py:227
  3260.4 1148.5 %copy-start.50 = (f32[204544]{0:T(1024)S(1)}, f32[204544]{0:T(1024)}, u32[]{:S(2)}) copy-start(f32[204544]{0:T(1024)} %param.20) | copy-start | bytes 2454532
  3260.4 1148.5 %copy-start.88 = (f32[204544]{0:T(1024)S(1)}, f32[204544]{0:T(1024)}, u32[]{:S(2)}) copy-start(f32[204544]{0:T(1024)} %param.23) | copy-start | bytes 2454532
  3260.4 1148.5 %copy-start.89 = (f32[204544]{0:T(1024)S(1)}, f32[204544]{0:T(1024)}, u32[]{:S(2)}) copy-start(f32[204544]{0:T(1024)} %param.22) | copy-start | bytes 2454532
  3260.4 1148.5 %copy-start.90 = (f32[204544]{0:T(1024)S(1)}, f32[204544]{0:T(1024)}, u32[]{:S(2)}) copy-start(f32[204544]{0:T(1024)} %param.21) | copy-start | bytes 2454532
  (211 other events, 2296.0 us)
Sparse Core Ops, SparseCore 0:
  14.0 162.4 all-gather.2
